TPU v7x, 32 devices: a whole 2x2x4 slice. The times are simulated.
32 devices in a mesh: pix: 8 (over z, y), rep: 4 (over x, core).
Axes of the slice: x: 2, y: 2, z: 4, core: 2. Of those that a mesh axis runs over, the one named last changes fastest.
Arguments:
- sky_cube: float32 [4, 512, 65536], P('rep', None, 'pix'), may hold values from -6 to 10
- pixel_mask: int32 [4, 65536], P('rep', 'pix'), may hold values 0 or 1
- noise_cov: float32 [512, 512], replicated, may hold values from -1 to 2, as said below
Outputs:
- power_cube: float32 [4, 512, 65536], P('rep', 'pix')
Inputs may be any that keep to these rules, and one draw needn't show every extreme that they name: `noise_cov`: symmetric; each diagonal entry exceeds the sum of magnitudes off the diagonal in its row.
All inputs are finite; a program needn't handle non-finite values. No bound on the sum of `pixel_mask` on one device may be relied on, other than what follows from the above.
Results may differ from a plain program's by a relative error of at most 0.00012.
Values sent between devices are 32-bit elements; how exact they have to be, the bound alone decides.
A program may use at most 320 MiB of HBM per device.

v0:
```python
import math
import jax
import jax.numpy as jnp
from jax import lax
from jax.sharding import PartitionSpec as P

F = 512
SY = 256
SX = 256
HI = lax.Precision.HIGHEST


def dft_pair(length):
    idx = jnp.arange(length, dtype=jnp.int32)
    phase = (idx[:, None] * idx[None, :] % length).astype(jnp.float32) * (2.0 * math.pi / length)
    return (jnp.cos(phase), jnp.sin(phase))


def los_table(length):
    idx = jnp.arange(length, dtype=jnp.int32)
    half_len = length // 2
    freq = jnp.where(idx <= half_len, idx, idx - half_len)
    phase = (freq[:, None] * idx[None, :] % length).astype(jnp.float32) * (2.0 * math.pi / length)
    values = jnp.where((idx <= half_len)[:, None], jnp.cos(phase), jnp.sin(phase))
    edge = jnp.logical_or(idx == 0, idx == half_len)
    scale = jnp.where(edge, math.sqrt(1.0 / length), math.sqrt(2.0 / length)).astype(jnp.float32)
    return values * scale[:, None]


def sky_power(planes, rows_y, cols_x):
    count = planes.shape[0]
    field = planes.reshape(count, rows_y, cols_x)
    cos_x, sin_x = dft_pair(cols_x)
    cos_y, sin_y = dft_pair(rows_y)
    both_x = jnp.concatenate([cos_x, sin_x], axis=1)
    both_y = jnp.concatenate([cos_y, sin_y], axis=0)
    first = jnp.einsum("kyx,xw->kyw", field, both_x, precision=HI)
    second = jnp.einsum("vy,kyw->kvw", both_y, first, precision=HI)
    real_part = second[:, :rows_y, :cols_x] - second[:, rows_y:, cols_x:]
    imag_part = -(second[:, rows_y:, :cols_x] + second[:, :rows_y, cols_x:])
    power_map = (real_part * real_part + imag_part * imag_part) / float(rows_y * cols_x)
    return power_map.reshape(count, rows_y * cols_x)


def reduce_cov(partial_value):
    summed = lax.psum(partial_value, ("pix", "rep"))
    return summed


def plane_power(planes):
    return sky_power(planes[0], SY, SX)[None]


def local(sky_cube, pixel_mask, noise_cov):
    live = pixel_mask[0].astype(jnp.float32)
    masked = sky_cube[0] * live[None, :]
    table = los_table(F)
    partial_value = jnp.dot(masked, masked.T, precision=HI)
    data_cov = reduce_cov(partial_value)
    scale_all = float(lax.axis_size("pix") * lax.axis_size("rep") * masked.shape[1])
    regular = data_cov / scale_all + noise_cov
    factor = jnp.linalg.cholesky(regular)
    filter_t = jax.scipy.linalg.cho_solve((factor, True), noise_cov)
    folded_map = jnp.dot(table, filter_t.T, precision=HI)
    spectra = jnp.dot(folded_map, masked, precision=HI)
    owners = lax.axis_size("pix")
    stacked = spectra.reshape(owners, spectra.shape[0] // owners, spectra.shape[1])
    return plane_power(lax.all_to_all(stacked, "pix", split_axis=0, concat_axis=2, tiled=True))


def solution(mesh):
    placed = (P("rep", None, "pix"), P("rep", "pix"), P())
    return jax.shard_map(
        local, mesh=mesh, in_specs=placed, out_specs=P("rep", "pix", None), check_vma=False
    )
```

profile of v0, /device:TPU:0, one launch (start us, length us, event | category | flops | bytes accessed | tf_op | source)
XLA Modules:
  0.0 922.2 jit_solution(2023043148262930889)
XLA Ops:
  6.5 0.8 convert_element_type.18
  7.3 32.8 %fusion.6 = f32[512,512]{0,1:T(8,128)} fusion(f32[1,512,8192]{2,1,0:T(8,128)} %param.3, f32[8192]{0:T(1024)S(1)} %bitcast.88), kind=kOutput, calls=%fused_computation.11 | convolution fusion | flops 25773998080 | bytes 17858560 | tf_op jit(solution)/shard_map/dot_general | solution.py:58
  40.5 133.3 %all-reduce.3.cloned.1.call-done = f32[512,512]{0,1:T(8,128)} async-done(((f32[512,512]{0,1:T(8,128)}), f32[512,512]{0,1:T(8,128)}) %all-reduce.3.cloned.1.call-update) | async-done | bytes 1048592 | tf_op jit(solution)/shard_map/psum | solution.py:46
  173.8 1.4 multiply_add_fusion
  175.8 1.0 copy-done.1
  176.8 11.7 %cholesky.104 = f32[128,128]{1,0:T(8,128)S(1)} custom-call(f32[128,128]{1,0:T(8,128)S(1)} %cholesky.266), custom_call_target="Cholesky" | custom-call | tf_op jit(solution)/shard_map/jit(cholesky)/cholesky | solution.py:62
  188.5 9.8 %custom-call.34 = f32[1,128,128]{1,2,0:T(8,128)S(1)} custom-call(f32[1,128,128]{2,1,0:T(8,128)S(1)} %get-tuple-element.32), custom_call_target="InvertDiagBlocksLowerTriangular" | custom-call | tf_op jit(solution)/shard_map/jit(cholesky)/cholesky | solution.py:62
  198.5 1.2 constant_dynamic-update-slice_fusion.2
  199.7 1.3 convolution_subtract_fusion.6
  201.0 11.7 %cholesky.217 = f32[128,128]{1,0:T(8,128)S(1)} custom-call(f32[128,128]{1,0:T(8,128)S(1)} %cholesky.270), custom_call_target="Cholesky" | custom-call | tf_op jit(solution)/shard_map/jit(cholesky)/cholesky | solution.py:62
  212.8 10.0 %custom-call.35 = f32[1,128,128]{1,2,0:T(8,128)S(1)} custom-call(f32[1,128,128]{2,1,0:T(8,128)S(1)} %get-tuple-element.29), custom_call_target="InvertDiagBlocksLowerTriangular" | custom-call | tf_op jit(solution)/shard_map/jit(cholesky)/cholesky | solution.py:62
  223.0 1.3 convolution_subtract_fusion.7
  224.3 11.7 %cholesky.238 = f32[128,128]{1,0:T(8,128)S(1)} custom-call(f32[128,128]{1,0:T(8,128)S(1)} %cholesky.275), custom_call_target="Cholesky" | custom-call | tf_op jit(solution)/shard_map/jit(cholesky)/cholesky | solution.py:62
  236.1 0.7 compare_reduce_fusion.1
  236.8 9.8 %custom-call.36 = f32[1,128,128]{1,2,0:T(8,128)S(1)} custom-call(f32[1,128,128]{2,1,0:T(8,128)S(1)} %get-tuple-element.26), custom_call_target="InvertDiagBlocksLowerTriangular" | custom-call | tf_op jit(solution)/shard_map/jit(cholesky)/cholesky | solution.py:62
  246.8 1.2 convolution_subtract_fusion.8
  248.0 12.1 %cholesky.255 = f32[128,128]{1,0:T(8,128)S(1)} custom-call(f32[128,128]{1,0:T(8,128)S(1)} %convolution_subtract_fusion.8), custom_call_target="Cholesky" | custom-call | tf_op jit(solution)/shard_map/jit(cholesky)/cholesky | solution.py:62
  260.2 0.6 compare_reduce_fusion
  260.8 0.7 compare_reduce_fusion.2
  264.1 8.5 while.1
  264.2 0.6 fusion.126
  264.8 1.4 bitcast_dynamic-update-slice_fusion.2
  266.3 0.6 fusion.126
  266.9 1.4 bitcast_dynamic-update-slice_fusion.2
  268.5 0.6 fusion.126
  269.1 1.4 bitcast_dynamic-update-slice_fusion.2
  270.6 0.6 fusion.126
  271.2 1.4 bitcast_dynamic-update-slice_fusion.2
  272.6 39.3 %custom-call.37 = f32[4,128,128]{1,2,0:T(8,128)S(1)} custom-call(f32[4,128,128]{2,1,0:T(8,128)S(1)} %get-tuple-element.12), custom_call_target="InvertDiagBlocksLowerTriangular" | custom-call | tf_op jit(solution)/shard_map/jit(_cho_solve)/triangular_solve | solution.py:63
  312.0 0.4 fusion.68
  312.8 0.4 fusion.91
  313.2 0.4 convolution_subtract_fusion.2
  314.0 0.6 convolution_subtract_fusion.5
  315.5 0.4 convolution_subtract_fusion.1
  316.3 0.5 convolution_subtract_fusion
  317.1 0.7 convolution_subtract_fusion.4
  318.2 6.1 fusion.15
  324.3 31.8 %fusion.4 = f32[8,64,8192]{2,1,0:T(8,128)} fusion(f32[8,64,512]{2,1,0:T(8,128)S(1)} %bitcast.87, f32[1,512,8192]{2,1,0:T(8,128)} %param.3, f32[8192]{0:T(1024)S(1)} %bitcast.89), kind=kOutput, calls=%fused_computation.9 | convolution fusion | flops 25773998080 | bytes 34635776 | tf_op jit(solution)/shard_map/dot_general | solution.py:65
  356.1 5.8 all-to-all-start
  361.9 1.0 fusion.80
  363.0 361.2 %all-to-all-done = f32[8,64,8192]{2,1,0:T(8,128)} async-done(((f32[8,64,8192]{2,1,0:T(8,128)}), f32[8,64,8192]{2,1,0:T(8,128)}, u32[]{:S(2)}, u32[]{:S(2)}) %all-to-all-start) | async-done | bytes 16777248 | tf_op jit(solution)/shard_map/all_to_all | solution.py:68
  724.1 17.8 %copy.10 = f32[1,64,8,8192]{3,2,1,0:T(8,128)} copy(f32[1,64,8,8192]{3,1,2,0:T(8,128)} %bitcast.16) | data formatting | bytes 33554432 | tf_op jit(solution)/shard_map/all_to_all | solution.py:68
  741.9 18.0 %reshape_squeeze.3 = f32[64,256,256]{2,1,0:T(8,128)} reshape(f32[1,64,8,8192]{3,2,1,0:T(8,128)} %copy.10) | data formatting | bytes 33554432 | tf_op jit(solution)/shard_map/reshape;squeeze | solution.py:32
  759.9 33.4 %fusion.50 = f32[64,256,512]{1,2,0:T(8,128)} fusion(f32[64,256,256]{2,1,0:T(8,128)} %reshape_squeeze.3, f32[256,256]{1,0:T(8,128)S(1)} %get-tuple-element.37, f32[256,256]{1,0:T(8,128)S(1)} %get-tuple-element.38), kind=kOutput, calls=%fused_computation.71 | convolution fusion | flops 25769934848 | bytes 50855936 | tf_op jit(solution)/shard_map/kyx,xw->kyw/dot_general | solution.py:37
  793.3 61.2 %convolution_bitcast_fusion = f32[64,512,512]{1,2,0:T(8,128)} fusion(f32[64,256,512]{1,2,0:T(8,128)} %fusion.50, f32[512,256,1]{1,0,2:T(8,128)S(1)} %maximum_bitcast_fusion.6), kind=kOutput, calls=%fused_computation.2 | convolution fusion | flops 51539607552 | bytes 101187584 | tf_op jit(solution)/shard_map/vy,kyw->kvw/dot_general | solution.py:38
  854.5 28.6 %fusion.2 = f32[64,256,256]{1,2,0:T(8,128)} fusion(f32[64,512,512]{1,2,0:T(8,128)} %convolution_bitcast_fusion), kind=kLoop, calls=%fused_computation.6 | loop fusion | flops 25165824 | bytes 83886080 | tf_op jit(solution)/shard_map/div | solution.py:41
  883.1 17.5 %copy.11 = f32[64,256,256]{2,1,0:T(8,128)} copy(f32[64,256,256]{1,2,0:T(8,128)} %fusion.2) | data formatting | bytes 33554432 | tf_op jit(solution)/shard_map/div | solution.py:41
  900.5 14.6 %broadcast_in_dim_reshape.3 = f32[1,64,65536]{2,1,0:T(8,128)} reshape(f32[64,256,256]{2,1,0:T(8,128)} %copy.11) | data formatting | bytes 33554432 | tf_op jit(solution)/shard_map/broadcast_in_dim;reshape | solution.py:51
  (37 shorter events, 4.8 us)
Async XLA Ops:
  6.5 167.3 %all-reduce.3.cloned.1.call-start = ((), (), s32[]{:S(2)}) async-start(), calls=%async_computation.1 | async-start | bytes 2097152 | tf_op jit(solution)/shard_map/psum | solution.py:46
  7.3 32.8 %copy-start = (f32[512,512]{1,0:T(8,128)S(1)}, f32[512,512]{1,0:T(8,128)}, u32[]{:S(2)}) copy-start(f32[512,512]{1,0:T(8,128)} %param.5) | copy-start | bytes 3145732
  175.8 1.0 copy-start.1
  356.1 368.0 %all-to-all-start = ((f32[8,64,8192]{2,1,0:T(8,128)}), f32[8,64,8192]{2,1,0:T(8,128)}, u32[]{:S(2)}, u32[]{:S(2)}) async-start(f32[8,64,8192]{2,1,0:T(8,128)} %fusion.4), calls=%async_computation | async-start | bytes 33554432 | tf_op jit(solution)/shard_map/all_to_all | solution.py:68
Sparse Core Ops, SparseCore 0:
  40.2 133.4 all-reduce.2
where the time goes:
time: 929 us; the launch traced here: 922 us
  waiting for transfers between devices  494 us (53%)
  matrix products  177 us (19%)
  other arithmetic  151 us (16%)
  local copies, waits for them, and re-layouts  78 us (8%)
  between operations  16.6 us (2%)
    all_to_all x1, waiting for transfers between devices, local(): lax.all_to_all(stacked, 'pix', split_axis=0, concat_axis=2, tiled=True)  361 us
    psum x1, waiting for transfers between devices, reduce_cov(): summed = lax.psum(partial_value, ('pix', 'rep'))  133 us
    another operation x14, other arithmetic, local(): factor = jnp.linalg.cholesky(regular)  79 us
    dot_general x1, matrix products, sky_power(): second = jnp.einsum('vy,kyw->kvw', both_y, first, precision=HI)  61.2 us
    another operation x3, other arithmetic, local(): filter_t = jax.scipy.linalg.cho_solve((factor, True), noise_cov)  39.4 us
    dot_general x1, matrix products, sky_power(): first = jnp.einsum('kyx,xw->kyw', field, both_x, precision=HI)  33.4 us
    dot_general x1, matrix products, local(): partial_value = jnp.dot(masked, masked.T, precision=HI)  32.8 us
    dot_general x1, matrix products, local(): spectra = jnp.dot(folded_map, masked, precision=HI)  31.8 us
  transfers between devices with their start and end apart: 2, of which 2 were waited for; matrix products, arithmetic and copies ran while one was open for 0% of the time, Pallas kernels for 0%

commit v1 on v0

--- a/solution.py
+++ b/solution.py
@@ -43,7 +43,8 @@
 
 
 def reduce_cov(partial_value):
-    summed = lax.psum(partial_value, ("pix", "rep"))
+    one_axis = lax.psum(partial_value, "rep")
+    summed = lax.psum(one_axis, "pix")
     return summed
 
 

time: 929 us -> 917 us (0.987)
  waiting for transfers between devices: 494 us -> 483 us
    psum x1 -> x2, waiting for transfers between devices: 133 us -> 121 us  [the longest x1 81.9 us: reduce_cov(): summed = lax.psum(one_axis, 'pix')]
  transfers between devices with their start and end apart: 2 -> 3, of which waited for: 2 -> 3; matrix products, arithmetic and copies ran while one was open for 0% -> 0% of each run, Pallas kernels for 0% -> 0%
where the time goes in v1:
time: 917 us; the launch traced here: 910 us
  waiting for transfers between devices  483 us (53%)
  matrix products  176 us (19%)
  other arithmetic  151 us (16%)
  local copies, waits for them, and re-layouts  78 us (9%)
  between operations  16.6 us (2%)
    all_to_all x1, waiting for transfers between devices, local(): lax.all_to_all(stacked, 'pix', split_axis=0, concat_axis=2, tiled=True)  362 us
    psum x1, waiting for transfers between devices, reduce_cov(): summed = lax.psum(one_axis, 'pix')  81.9 us
    another operation x14, other arithmetic, local(): factor = jnp.linalg.cholesky(regular)  79 us
    dot_general x1, matrix products, sky_power(): second = jnp.einsum('vy,kyw->kvw', both_y, first, precision=HI)  61.2 us
    another operation x3, other arithmetic, local(): filter_t = jax.scipy.linalg.cho_solve((factor, True), noise_cov)  39.4 us
    psum x1, waiting for transfers between devices, reduce_cov(): one_axis = lax.psum(partial_value, 'rep')  38.7 us
    dot_general x1, matrix products, sky_power(): first = jnp.einsum('kyx,xw->kyw', field, both_x, precision=HI)  33.4 us
    dot_general x1, matrix products, local(): partial_value = jnp.dot(masked, masked.T, precision=HI)  32.3 us
  transfers between devices with their start and end apart: 3, of which 3 were waited for; matrix products, arithmetic and copies ran while one was open for 0% of the time, Pallas kernels for 0%

profile of v1, /device:TPU:0, one launch (start us, length us, event | category | flops | bytes accessed | tf_op | source)
XLA Modules:
  0.0 910.4 jit_solution(17190444218025766808)
XLA Ops:
  6.5 0.8 convert_element_type.18
  7.3 32.3 %fusion.6 = f32[512,512]{0,1:T(8,128)} fusion(f32[1,512,8192]{2,1,0:T(8,128)} %param.3, f32[8192]{0:T(1024)S(1)} %bitcast.88), kind=kOutput, calls=%fused_computation.11 | convolution fusion | flops 25773998080 | bytes 17858560 | tf_op jit(solution)/shard_map/dot_general | solution.py:59
  39.7 0.5 all-reduce.6.cloned.1.call-start
  40.2 38.7 %all-reduce.4.cloned.1.call-done = f32[512,512]{0,1:T(8,128)} async-done(((f32[512,512]{0,1:T(8,128)}), f32[512,512]{0,1:T(8,128)}) %all-reduce.4.cloned.1.call-update) | async-done | bytes 1048592 | tf_op jit(solution)/shard_map/psum | solution.py:46
  79.3 81.9 %all-reduce.6.cloned.1.call-done = f32[512,512]{0,1:T(8,128)} async-done(((f32[512,512]{0,1:T(8,128)}), f32[512,512]{0,1:T(8,128)}) %all-reduce.6.cloned.1.call-update) | async-done | bytes 1048592 | tf_op jit(solution)/shard_map/psum | solution.py:47
  161.2 1.4 multiply_add_fusion
  163.2 1.0 copy-done.1
  164.2 11.7 %cholesky.104 = f32[128,128]{1,0:T(8,128)S(1)} custom-call(f32[128,128]{1,0:T(8,128)S(1)} %cholesky.266), custom_call_target="Cholesky" | custom-call | tf_op jit(solution)/shard_map/jit(cholesky)/cholesky | solution.py:63
  175.9 9.8 %custom-call.34 = f32[1,128,128]{1,2,0:T(8,128)S(1)} custom-call(f32[1,128,128]{2,1,0:T(8,128)S(1)} %get-tuple-element.32), custom_call_target="InvertDiagBlocksLowerTriangular" | custom-call | tf_op jit(solution)/shard_map/jit(cholesky)/cholesky | solution.py:63
  185.9 1.2 constant_dynamic-update-slice_fusion.2
  187.1 1.3 convolution_subtract_fusion.6
  188.4 11.7 %cholesky.217 = f32[128,128]{1,0:T(8,128)S(1)} custom-call(f32[128,128]{1,0:T(8,128)S(1)} %cholesky.270), custom_call_target="Cholesky" | custom-call | tf_op jit(solution)/shard_map/jit(cholesky)/cholesky | solution.py:63
  200.2 10.0 %custom-call.35 = f32[1,128,128]{1,2,0:T(8,128)S(1)} custom-call(f32[1,128,128]{2,1,0:T(8,128)S(1)} %get-tuple-element.29), custom_call_target="InvertDiagBlocksLowerTriangular" | custom-call | tf_op jit(solution)/shard_map/jit(cholesky)/cholesky | solution.py:63
  210.4 1.3 convolution_subtract_fusion.7
  211.7 11.7 %cholesky.238 = f32[128,128]{1,0:T(8,128)S(1)} custom-call(f32[128,128]{1,0:T(8,128)S(1)} %cholesky.275), custom_call_target="Cholesky" | custom-call | tf_op jit(solution)/shard_map/jit(cholesky)/cholesky | solution.py:63
  223.4 0.7 compare_reduce_fusion.1
  224.2 9.8 %custom-call.36 = f32[1,128,128]{1,2,0:T(8,128)S(1)} custom-call(f32[1,128,128]{2,1,0:T(8,128)S(1)} %get-tuple-element.26), custom_call_target="InvertDiagBlocksLowerTriangular" | custom-call | tf_op jit(solution)/shard_map/jit(cholesky)/cholesky | solution.py:63
  234.2 1.2 convolution_subtract_fusion.8
  235.4 12.1 %cholesky.255 = f32[128,128]{1,0:T(8,128)S(1)} custom-call(f32[128,128]{1,0:T(8,128)S(1)} %convolution_subtract_fusion.8), custom_call_target="Cholesky" | custom-call | tf_op jit(solution)/shard_map/jit(cholesky)/cholesky | solution.py:63
  247.6 0.6 compare_reduce_fusion
  248.2 0.7 compare_reduce_fusion.2
  251.5 8.5 while.1
  251.6 0.6 fusion.126
  252.2 1.4 bitcast_dynamic-update-slice_fusion.2
  253.7 0.6 fusion.126
  254.3 1.4 bitcast_dynamic-update-slice_fusion.2
  255.9 0.6 fusion.126
  256.5 1.4 bitcast_dynamic-update-slice_fusion.2
  258.0 0.6 fusion.126
  258.6 1.4 bitcast_dynamic-update-slice_fusion.2
  260.0 39.3 %custom-call.37 = f32[4,128,128]{1,2,0:T(8,128)S(1)} custom-call(f32[4,128,128]{2,1,0:T(8,128)S(1)} %get-tuple-element.12), custom_call_target="InvertDiagBlocksLowerTriangular" | custom-call | tf_op jit(solution)/shard_map/jit(_cho_solve)/triangular_solve | solution.py:64
  300.6 0.4 convolution_subtract_fusion.2
  301.4 0.6 convolution_subtract_fusion.5
  302.9 0.4 convolution_subtract_fusion.1
  303.7 0.5 convolution_subtract_fusion
  304.5 0.7 convolution_subtract_fusion.4
  305.6 6.1 fusion.15
  311.7 31.8 %fusion.4 = f32[8,64,8192]{2,1,0:T(8,128)} fusion(f32[8,64,512]{2,1,0:T(8,128)S(1)} %bitcast.87, f32[1,512,8192]{2,1,0:T(8,128)} %param.3, f32[8192]{0:T(1024)S(1)} %bitcast.89), kind=kOutput, calls=%fused_computation.9 | convolution fusion | flops 25773998080 | bytes 34635776 | tf_op jit(solution)/shard_map/dot_general | solution.py:66
  343.5 5.8 all-to-all-start
  349.3 1.0 fusion.80
  350.3 362.0 %all-to-all-done = f32[8,64,8192]{2,1,0:T(8,128)} async-done(((f32[8,64,8192]{2,1,0:T(8,128)}), f32[8,64,8192]{2,1,0:T(8,128)}, u32[]{:S(2)}, u32[]{:S(2)}) %all-to-all-start) | async-done | bytes 16777248 | tf_op jit(solution)/shard_map/all_to_all | solution.py:69
  712.3 17.8 %copy.10 = f32[1,64,8,8192]{3,2,1,0:T(8,128)} copy(f32[1,64,8,8192]{3,1,2,0:T(8,128)} %bitcast.16) | data formatting | bytes 33554432 | tf_op jit(solution)/shard_map/all_to_all | solution.py:69
  730.1 18.0 %reshape_squeeze.3 = f32[64,256,256]{2,1,0:T(8,128)} reshape(f32[1,64,8,8192]{3,2,1,0:T(8,128)} %copy.10) | data formatting | bytes 33554432 | tf_op jit(solution)/shard_map/reshape;squeeze | solution.py:32
  748.1 33.4 %fusion.50 = f32[64,256,512]{1,2,0:T(8,128)} fusion(f32[64,256,256]{2,1,0:T(8,128)} %reshape_squeeze.3, f32[256,256]{1,0:T(8,128)S(1)} %get-tuple-element.37, f32[256,256]{1,0:T(8,128)S(1)} %get-tuple-element.38), kind=kOutput, calls=%fused_computation.71 | convolution fusion | flops 25769934848 | bytes 50855936 | tf_op jit(solution)/shard_map/kyx,xw->kyw/dot_general | solution.py:37
  781.5 61.2 %convolution_bitcast_fusion = f32[64,512,512]{1,2,0:T(8,128)} fusion(f32[64,256,512]{1,2,0:T(8,128)} %fusion.50, f32[512,256,1]{1,0,2:T(8,128)S(1)} %maximum_bitcast_fusion.6), kind=kOutput, calls=%fused_computation.2 | convolution fusion | flops 51539607552 | bytes 101187584 | tf_op jit(solution)/shard_map/vy,kyw->kvw/dot_general | solution.py:38
  842.7 28.6 %fusion.2 = f32[64,256,256]{1,2,0:T(8,128)} fusion(f32[64,512,512]{1,2,0:T(8,128)} %convolution_bitcast_fusion), kind=kLoop, calls=%fused_computation.6 | loop fusion | flops 25165824 | bytes 83886080 | tf_op jit(solution)/shard_map/div | solution.py:41
  871.3 17.5 %copy.11 = f32[64,256,256]{2,1,0:T(8,128)} copy(f32[64,256,256]{1,2,0:T(8,128)} %fusion.2) | data formatting | bytes 33554432 | tf_op jit(solution)/shard_map/div | solution.py:41
  888.7 14.6 %broadcast_in_dim_reshape.3 = f32[1,64,65536]{2,1,0:T(8,128)} reshape(f32[64,256,256]{2,1,0:T(8,128)} %copy.11) | data formatting | bytes 33554432 | tf_op jit(solution)/shard_map/broadcast_in_dim;reshape | solution.py:52
  (40 shorter events, 5.7 us)
Async XLA Ops:
  6.5 72.3 %all-reduce.4.cloned.1.call-start = ((), (), s32[]{:S(2)}) async-start(), calls=%async_computation.1 | async-start | bytes 2097152 | tf_op jit(solution)/shard_map/psum | solution.py:46
  7.3 71.6 %copy-start = (f32[512,512]{1,0:T(8,128)S(1)}, f32[512,512]{1,0:T(8,128)}, u32[]{:S(2)}) copy-start(f32[512,512]{1,0:T(8,128)} %param.5) | copy-start | bytes 3145732
  39.7 121.5 %all-reduce.6.cloned.1.call-start = ((), (), s32[]{:S(2)}) async-start(), calls=%async_computation.2 | async-start | bytes 2097152 | tf_op jit(solution)/shard_map/psum | solution.py:47
  163.2 1.0 copy-start.1
  343.5 368.8 %all-to-all-start = ((f32[8,64,8192]{2,1,0:T(8,128)}), f32[8,64,8192]{2,1,0:T(8,128)}, u32[]{:S(2)}, u32[]{:S(2)}) async-start(f32[8,64,8192]{2,1,0:T(8,128)} %fusion.4), calls=%async_computation | async-start | bytes 33554432 | tf_op jit(solution)/shard_map/all_to_all | solution.py:69
Sparse Core Ops, SparseCore 0:
  39.8 39.0 all-reduce.3
  82.4 78.7 all-reduce.5
